TPU v7x, 256 devices: a whole 4x4x8 slice. The times are simulated.
256 devices in a mesh: doc: 64 (over z, y, core), feat: 4 (over x).
Axes of the slice: x: 4, y: 4, z: 8, core: 2. Of those that a mesh axis runs over, the one named last changes fastest.
Arguments:
- scores: float32 [768, 128], P('doc'), may hold values from -6 to 6
- clicks: int32 [768, 128], P('doc'), may hold values from 0 to 1, as said below
- lengths: int32 [768], P('doc'), may hold values from 2 to 128, as said below
- t_plus_old: float32 [128], replicated, may hold values from 0.1 to 1
- t_minus_old: float32 [128], replicated, may hold values from 0.1 to 1
- leaf: int32 [98304], P('doc'), may hold values from 0 to 31
- bins: int32 [512, 98304], P('feat', 'doc'), may hold values from 0 to 255
Outputs:
- t_plus: float32 [128], replicated
- t_minus: float32 [128], replicated
- gradients: float32 [2, 98304], P(None, 'doc')
- hist: float32 [512, 64, 256], P(('feat', 'doc'))
Inputs may be any that keep to these rules, and one draw needn't show every extreme that they name: Query q shows its first lengths[q] slots; the first two queries of each block of 12 queries show all 128. `clicks`: values at or beyond a query's length carry no meaning. In the first query of each block of 12 queries the even positions are clicked and the odd ones not; in the second the reverse.
All inputs are finite; a program needn't handle non-finite values.
Results may differ from a plain program's by a relative error of at most 0.0024.
Values may be sent and summed in bfloat16 or wider, within the bound.
No kernel may reach another device: no remote copies, remote signals or barrier semaphores. Data moves between devices by JAX's collectives and lax.ppermute only.
A program may use at most 64 MiB of HBM per device.

v0:
```python
import jax
import jax.numpy as jnp
from jax import lax
from jax.sharding import PartitionSpec as P

BINS = 256
LEAVES = 32


def pair_terms(scores, clicks, lengths, t_plus_old, t_minus_old):
    npos = scores.shape[1]
    places = jnp.arange(npos)
    shown_mask = places[None, :] < lengths[:, None]
    clicked = jnp.where((clicks == 1) & shown_mask, 1.0, 0.0).astype(jnp.float32)
    skipped = jnp.where((clicks == 0) & shown_mask, 1.0, 0.0).astype(jnp.float32)
    paired = clicked[:, :, None] * skipped[:, None, :]
    discount = 1.0 / jnp.log2(2.0 + places.astype(jnp.float32))
    clicks_count = jnp.sum(clicked, axis=1)
    ideal_gain = jnp.sum(
        jnp.where(
            places[None, :].astype(jnp.float32) < clicks_count[:, None], discount[None, :], 0.0
        ),
        axis=1,
    )
    ideal_gain = jnp.maximum(ideal_gain, 1.0)
    change = (
        paired * jnp.abs(discount[:, None] - discount[None, :])[None] / ideal_gain[:, None, None]
    )
    spread = scores[:, :, None] - scores[:, None, :]
    weighted = change * jax.nn.softplus(-spread)
    plus_part = jnp.sum(weighted / t_minus_old[None, None, :], axis=(0, 2))
    minus_part = jnp.sum(weighted / t_plus_old[None, :, None], axis=(0, 1))
    return (change, spread, plus_part, minus_part)


def lambda_rows(change, spread, plus_sum, minus_sum):
    t_plus = jnp.sqrt(plus_sum / plus_sum[0])
    t_minus = jnp.sqrt(minus_sum / minus_sum[0])
    scaled = change / (t_plus[None, :, None] * t_minus[None, None, :])
    chance = jax.nn.sigmoid(-spread)
    lambda_pair = scaled * chance
    second = lambda_pair * (1.0 - chance)
    slopes = jnp.sum(lambda_pair, axis=1) - jnp.sum(lambda_pair, axis=2)
    curvature = jnp.sum(second, axis=1) + jnp.sum(second, axis=2)
    own_rows = jnp.stack([slopes.reshape(-1), curvature.reshape(-1)])
    return (t_plus, t_minus, own_rows)


def leaf_weights(slope_row, curve_row, leaf_row):
    leaf_hit = (leaf_row[None, :] == jnp.arange(LEAVES)[:, None]).astype(jnp.bfloat16)
    return jnp.concatenate([leaf_hit * slope_row[None, :], leaf_hit * curve_row[None, :]], axis=0)


def block_hist(bin_rows, weights, levels):
    one_hot = (bin_rows[:, None, :] == levels[None, :, None]).astype(jnp.bfloat16)
    return jnp.einsum("gr,nbr->ngb", weights, one_hot, preferred_element_type=jnp.float32)


def feature_hist(bin_rows, weights):
    levels = jnp.arange(BINS, dtype=jnp.int32)
    row_count = bin_rows.shape[0]
    block_size = 1
    for option in (8, 4, 2):
        if block_size == 1 and row_count % option == 0:
            block_size = option

    def one_block(block):
        return block_hist(block, weights, levels)

    stacked = lax.map(
        one_block, bin_rows.reshape(row_count // block_size, block_size, bin_rows.shape[1])
    )
    return stacked.reshape(row_count, weights.shape[0], BINS)


def body(scores, clicks, lengths, t_plus_old, t_minus_old, leaf, bins):
    per_feat = scores.shape[0] // lax.axis_size("feat")
    start_row = lax.axis_index("feat") * per_feat
    my_scores = lax.dynamic_slice_in_dim(scores, start_row, per_feat, 0)
    my_clicks = lax.dynamic_slice_in_dim(clicks, start_row, per_feat, 0)
    my_lengths = lax.dynamic_slice_in_dim(lengths, start_row, per_feat, 0)
    change, spread, plus_part, minus_part = pair_terms(
        my_scores, my_clicks, my_lengths, t_plus_old, t_minus_old
    )
    plus_sum, minus_sum = lax.psum((plus_part, minus_part), ("doc", "feat"))
    t_plus, t_minus, own_rows = lambda_rows(change, spread, plus_sum, minus_sum)
    gradients = lax.all_gather(own_rows, "feat", axis=1, tiled=True)
    rounded = gradients.astype(jnp.bfloat16)
    weights = leaf_weights(rounded[0], rounded[1], leaf)
    hist = lax.psum_scatter(feature_hist(bins, weights), "doc", scatter_dimension=0, tiled=True)
    return (t_plus, t_minus, gradients, hist)


def solution(mesh):
    placed = (P("doc", None), P("doc", None), P("doc"), P(), P(), P("doc"), P("feat", "doc"))
    return jax.shard_map(
        body,
        mesh=mesh,
        in_specs=placed,
        out_specs=(P(), P(), P(None, "doc"), P(("feat", "doc"), None, None)),
        check_vma=False,
    )
```

profile of v0, /device:TPU:2, one launch (start us, length us, event | category | flops | bytes accessed | tf_op | source)
XLA Modules:
  0.0 321.2 jit_solution(5064826501937953063)
XLA Ops:
  8.1 0.9 fusion.26
  9.2 1.0 divide_reduce_fusion
  10.2 78.7 %all-reduce = (f32[128]{0:T(128)S(1)}, f32[128]{0:T(128)S(1)}) all-reduce(f32[128]{0:T(128)S(1)} %get-tuple-element.47, f32[128]{0:T(128)S(1)} %get-tuple-element.46), channel_id=1, replica_groups=mesh['doc'=64,'feat'=4] {'doc','feat'}, use_global_device_ids=true, to_apply=%region_3.4 | all-reduce | flops 256 | bytes 2048 | tf_op jit(solution)/shard_map/psum | solution.py:85
  89.4 12.0 %all_gather.3 = f32[2,1536]{1,0:T(2,128)S(1)} all-gather(f32[2,384]{1,0:T(2,128)S(1)} %pad_maximum_fusion.1), channel_id=1, replica_groups=mesh['doc'=64,'feat'=4] {'feat'}, dimensions={1}, use_global_device_ids=true | all-gather | bytes 15360 | tf_op jit(solution)/shard_map/all_gather | solution.py:87
  102.3 61.6 %while.11 = (s32[]{:T(128)}, f32[16,8,64,256]{3,2,1,0:T(8,128)}, s32[16,8,1536]{2,1,0:T(8,128)}, bf16[64,1536]{1,0:T(8,128)(2,1)S(1)}, s32[]{:T(128)}) while((s32[]{:T(128)}, f32[16,8,64,256]{3,2,1,0:T(8,128)}, s32[16,8,1536]{2,1,0:T(8,128)}, bf16[64,1536]{1,0:T(8,128)(2,1)S(1)}, s32[]{:T(128)}) %tuple.41), condition=%wide.region_11.12_spmd.clone, body=%wide.region_10.11_spmd.clone.sunk | while | flops 405798912 | bytes 868929 | solution.py:70
  102.3 0.8 dynamic-slice_bitcast_fusion.2
  103.1 3.0 fusion.31
  106.1 0.8 dynamic-slice_bitcast_fusion.2
  106.9 3.1 fusion.31
  110.8 3.1 fusion.31
  114.7 3.1 fusion.31
  118.5 3.0 fusion.31
  122.3 3.1 fusion.31
  126.2 3.0 fusion.31
  130.0 3.1 fusion.31
  133.9 3.0 fusion.31
  137.7 3.1 fusion.31
  141.6 3.0 fusion.31
  145.4 3.1 fusion.31
  149.3 3.0 fusion.31
  153.1 3.1 fusion.31
  157.0 3.0 fusion.31
  160.8 3.1 fusion.31
  163.9 149.9 %reduce-scatter.2.cloned.1.call-done = f32[2,64,256]{2,1,0:T(8,128)} async-done(((f32[128,64,256]{2,1,0:T(8,128)}), f32[2,64,256]{2,1,0:T(8,128)}) %reduce-scatter.2.cloned.1.call-update) | async-done | bytes 131088 | tf_op jit(solution)/shard_map/reduce_scatter | solution.py:90
  (41 shorter events, 14.2 us)
Async XLA Ops:
  7.2 306.6 %reduce-scatter.2.cloned.1.call-start = ((), (), s32[]{:S(2)}) async-start(), calls=%async_computation.1 | async-start | bytes 8519680 | tf_op jit(solution)/shard_map/reduce_scatter | solution.py:90
  88.9 13.4 %copy-start = (f32[128]{0:T(128)}, f32[128]{0:T(128)S(1)}, u32[]{:S(2)}) copy-start(f32[128]{0:T(128)S(1)} %divide_sqrt_fusion) | copy-start | bytes 1540
  88.9 13.3 %copy-start.1 = (f32[128]{0:T(128)}, f32[128]{0:T(128)S(1)}, u32[]{:S(2)}) copy-start(f32[128]{0:T(128)S(1)} %divide_sqrt_fusion.1) | copy-start | bytes 1540
Sparse Core Ops, SparseCore 0:
  164.0 149.6 reduce-scatter.1
where the time goes:
time: 322 us; the launch traced here: 321 us
  waiting for transfers between devices  150 us (47%)
  blocking collectives  90.7 us (28%)
  matrix products  48.7 us (15%)
  local copies, waits for them, and re-layouts  14.2 us (4%)
  between operations  14.2 us (4%)
  other arithmetic  3.45 us (1%)
    reduce_scatter x1, waiting for transfers between devices, body(): lax.psum_scatter(feature_hist(bins, weights), 'doc', scatter_dimension=0,...  150 us
    psum x1, blocking collectives, body(): plus_sum, minus_sum = lax.psum((plus_part, minus_part), ('doc', 'feat'))  78.7 us
    dot_general x16, matrix products, block_hist(): jnp.einsum('gr,nbr->ngb', weights, one_hot, preferred_element_type=jnp.fl...  48.7 us
    eq x16, local copies, waits for them, and re-layouts, block_hist(): bin_rows[:, None, :] == levels[None, :, None]  12.8 us
    all_gather x1, blocking collectives, body(): gradients = lax.all_gather(own_rows, 'feat', axis=1, tiled=True)  12 us
  transfers between devices with their start and end apart: 1, of which 1 were waited for; matrix products, arithmetic and copies ran while one was open for 0% of the time, Pallas kernels for 0%

commit v1 on v0

--- a/solution.py
+++ b/solution.py
@@ -74,6 +74,11 @@
 
 
 def body(scores, clicks, lengths, t_plus_old, t_minus_old, leaf, bins):
+
+    def divide_results(inputs, mesh_dim, ax_name):
+        left_arr = lax.psum(inputs, mesh_dim)
+        return lax.psum(left_arr, ax_name)
+
     per_feat = scores.shape[0] // lax.axis_size("feat")
     start_row = lax.axis_index("feat") * per_feat
     my_scores = lax.dynamic_slice_in_dim(scores, start_row, per_feat, 0)
@@ -82,7 +87,7 @@
     change, spread, plus_part, minus_part = pair_terms(
         my_scores, my_clicks, my_lengths, t_plus_old, t_minus_old
     )
-    plus_sum, minus_sum = lax.psum((plus_part, minus_part), ("doc", "feat"))
+    plus_sum, minus_sum = divide_results((plus_part, minus_part), "doc", "feat")
     t_plus, t_minus, own_rows = lambda_rows(change, spread, plus_sum, minus_sum)
     gradients = lax.all_gather(own_rows, "feat", axis=1, tiled=True)
     rounded = gradients.astype(jnp.bfloat16)

time: 322 us -> 382 us (1.19)
  blocking collectives: 90.7 us -> 152 us
    psum x1 -> x2, blocking collectives: 78.7 us -> 140 us  [the longest x1 132 us: divide_results(): left_arr = lax.psum(inputs, mesh_dim)]
where the time goes in v1:
time: 382 us; the launch traced here: 380 us
  blocking collectives  152 us (40%)
  waiting for transfers between devices  148 us (39%)
  matrix products  48.7 us (13%)
  local copies, waits for them, and re-layouts  14.2 us (4%)
  between operations  14.2 us (4%)
    reduce_scatter x1, waiting for transfers between devices, body(): lax.psum_scatter(feature_hist(bins, weights), 'doc', scatter_dimension=0,...  148 us
    psum x1, blocking collectives, divide_results(): left_arr = lax.psum(inputs, mesh_dim)  132 us
    dot_general x16, matrix products, block_hist(): jnp.einsum('gr,nbr->ngb', weights, one_hot, preferred_element_type=jnp.fl...  48.7 us
    eq x16, local copies, waits for them, and re-layouts, block_hist(): bin_rows[:, None, :] == levels[None, :, None]  12.8 us
    all_gather x1, blocking collectives, body(): gradients = lax.all_gather(own_rows, 'feat', axis=1, tiled=True)  11.2 us
    psum x1, blocking collectives, divide_results(): return lax.psum(left_arr, ax_name)  8.6 us
  transfers between devices with their start and end apart: 1, of which 1 were waited for; matrix products, arithmetic and copies ran while one was open for 0% of the time, Pallas kernels for 0%

profile of v1, /device:TPU:2, one launch (start us, length us, event | category | flops | bytes accessed | tf_op | source)
XLA Modules:
  0.0 380.5 jit_solution(9128182956396670990)
XLA Ops:
  8.1 0.9 fusion.26
  9.2 1.0 divide_reduce_fusion
  10.2 131.8 %all-reduce = (f32[128]{0:T(128)S(1)}, f32[128]{0:T(128)S(1)}) all-reduce(f32[128]{0:T(128)S(1)} %get-tuple-element.47, f32[128]{0:T(128)S(1)} %get-tuple-element.46), channel_id=1, replica_groups=mesh['doc'=64,'feat'=4] {'doc'}, use_global_device_ids=true, to_apply=%region_3.4 | all-reduce | flops 256 | bytes 2048 | tf_op jit(solution)/shard_map/psum | solution.py:79
  141.9 8.6 %all-reduce.1 = (f32[128]{0:T(128)S(1)}, f32[128]{0:T(128)S(1)}) all-reduce(f32[128]{0:T(128)S(1)} %get-tuple-element.58, f32[128]{0:T(128)S(1)} %get-tuple-element.59), channel_id=1, replica_groups=mesh['doc'=64,'feat'=4] {'feat'}, use_global_device_ids=true, to_apply=%region_4.5 | all-reduce | flops 256 | bytes 2048 | tf_op jit(solution)/shard_map/psum | solution.py:80
  151.2 11.2 %all_gather.3 = f32[2,1536]{1,0:T(2,128)S(1)} all-gather(f32[2,384]{1,0:T(2,128)S(1)} %pad_maximum_fusion.1), channel_id=1, replica_groups=mesh['doc'=64,'feat'=4] {'feat'}, dimensions={1}, use_global_device_ids=true | all-gather | bytes 15360 | tf_op jit(solution)/shard_map/all_gather | solution.py:92
  163.2 61.6 %while.11 = (s32[]{:T(128)}, f32[16,8,64,256]{3,2,1,0:T(8,128)}, s32[16,8,1536]{2,1,0:T(8,128)}, bf16[64,1536]{1,0:T(8,128)(2,1)S(1)}, s32[]{:T(128)}) while((s32[]{:T(128)}, f32[16,8,64,256]{3,2,1,0:T(8,128)}, s32[16,8,1536]{2,1,0:T(8,128)}, bf16[64,1536]{1,0:T(8,128)(2,1)S(1)}, s32[]{:T(128)}) %tuple.41), condition=%wide.region_13.14_spmd.clone, body=%wide.region_12.13_spmd.clone.sunk | while | flops 405798912 | bytes 868929 | solution.py:70
  163.2 0.8 dynamic-slice_bitcast_fusion.2
  164.0 3.0 fusion.31
  167.8 3.1 fusion.31
  171.7 3.1 fusion.31
  175.6 3.1 fusion.31
  179.4 3.0 fusion.31
  183.2 3.1 fusion.31
  187.1 3.0 fusion.31
  190.9 3.1 fusion.31
  194.8 3.0 fusion.31
  198.6 3.1 fusion.31
  202.5 3.0 fusion.31
  206.3 3.1 fusion.31
  210.2 3.0 fusion.31
  214.0 3.1 fusion.31
  217.9 3.0 fusion.31
  221.7 3.1 fusion.31
  224.8 148.2 %reduce-scatter.2.cloned.1.call-done = f32[2,64,256]{2,1,0:T(8,128)} async-done(((f32[128,64,256]{2,1,0:T(8,128)}), f32[2,64,256]{2,1,0:T(8,128)}) %reduce-scatter.2.cloned.1.call-update) | async-done | bytes 131088 | tf_op jit(solution)/shard_map/reduce_scatter | solution.py:95
  (42 shorter events, 15.0 us)
Async XLA Ops:
  7.2 365.9 %reduce-scatter.2.cloned.1.call-start = ((), (), s32[]{:S(2)}) async-start(), calls=%async_computation.1 | async-start | bytes 8519680 | tf_op jit(solution)/shard_map/reduce_scatter | solution.py:95
  150.6 12.6 %copy-start = (f32[128]{0:T(128)}, f32[128]{0:T(128)S(1)}, u32[]{:S(2)}) copy-start(f32[128]{0:T(128)S(1)} %divide_sqrt_fusion) | copy-start | bytes 1540
  150.7 12.5 %copy-start.1 = (f32[128]{0:T(128)}, f32[128]{0:T(128)S(1)}, u32[]{:S(2)}) copy-start(f32[128]{0:T(128)S(1)} %divide_sqrt_fusion.1) | copy-start | bytes 1540
Sparse Core Ops, SparseCore 0:
  224.9 148.0 reduce-scatter.1
